TPU v7x, 32 devices: a whole 2x2x4 slice. The times are simulated.
32 devices in a mesh: section: 4 (over y, core), outer: 2 (over x), inner: 4 (over z).
Axes of the slice: x: 2, y: 2, z: 4, core: 2. Of those that a mesh axis runs over, the one named last changes fastest.
Arguments:
- projected: bfloat16 [4, 1024, 1280], P('section', ('outer', 'inner')), may hold values from -64 to 64
- positions: int32 [1024], replicated, may hold values from 0 to 1023, as said below
- out_weight: bfloat16 [4, 1024, 16384], P('section', None, ('outer', 'inner')), may hold values from -1.5 to 1.5
- residual: bfloat16 [4, 1024, 16384], P('section', None, ('outer', 'inner')), may hold values from -8 to 8
- norm_gain: bfloat16 [4, 16384], P('section', ('outer', 'inner')), may hold values from 0.099609375 to 1.8984375
- next_weight: bfloat16 [4, 16384, 1280], P('section', ('outer', 'inner')), may hold values from -0.046875 to 0.046875
Outputs:
- next_projected: bfloat16 [4, 1024, 1280], P('section', ('outer', 'inner'))
- stream: bfloat16 [4, 1024, 16384], P('section', None, ('outer', 'inner'))
Inputs may be any that keep to these rules, and one draw needn't show every extreme that they name: Each aligned run of 64 stored tokens holds consecutive positions starting at a multiple of 64; every position 0 to 1023 is stored once.
All inputs are finite; a program needn't handle non-finite values.
Results may differ from a plain program's by a relative error of at most 0.023.
Values may be sent and summed in bfloat16 or wider, within the bound.
A program may use at most 128 MiB of HBM per device.

v0:
```python
import jax
import jax.numpy as jnp
from jax import lax
from jax.sharding import PartitionSpec as P

D = 16384
HQ = 8
HD = 128


def from_behind(value, axis, by):
    devices = lax.axis_size(axis)
    return lax.ppermute(value, axis, [(i, (i + by) % devices) for i in range(devices)])


def body(projected, positions, out_weight, residual, norm_gain, next_weight):
    local_rows = projected[0]
    tokens_here = local_rows.shape[0]
    shard_index = lax.axis_index(("outer", "inner"))
    query_positions = lax.dynamic_slice_in_dim(positions, shard_index * tokens_here, tokens_here)
    queries = local_rows[:, : HQ * HD].reshape(tokens_here, HQ, HD)
    key_value = local_rows[:, HQ * HD :]
    scale_factor = HD ** (-0.5)
    group_rows = lax.all_gather(key_value, "inner", axis=0, tiled=True)
    piece = lax.all_gather(group_rows, "outer", axis=0, tiled=True)
    running_max = jnp.full((HQ, tokens_here), -1e30, jnp.float32)
    keys = piece[:, :HD]
    values = piece[:, HD:]
    scores = (
        jnp.einsum("thd,jd->htj", queries, keys, preferred_element_type=jnp.float32) * scale_factor
    )
    visible = positions[None, None, :] <= query_positions[None, :, None]
    masked = jnp.where(visible, scores, -1e30)
    new_max = jnp.maximum(running_max, jnp.max(masked, axis=-1))
    weights = jnp.where(visible, jnp.exp(scores - new_max[..., None]), 0.0)
    new_total = jnp.sum(weights, axis=-1)
    mixed = jnp.einsum(
        "htj,jd->htd", weights.astype(jnp.bfloat16), values, preferred_element_type=jnp.float32
    )
    final_state = (new_max, new_total, mixed)
    final_max, final_total, final_acc = final_state
    attended = jnp.transpose(final_acc / final_total[..., None], (1, 0, 2))
    attended = attended.reshape(tokens_here, HQ * HD).astype(jnp.bfloat16)
    weight_out = out_weight[0]
    product = jnp.dot(
        lax.all_gather(attended, ("outer", "inner"), axis=0, tiled=True),
        weight_out,
        preferred_element_type=jnp.float32,
    )
    hidden = (residual[0].astype(jnp.float32) + product).astype(jnp.bfloat16)
    received = from_behind(hidden[None], "section", 1)
    stream_rows = received[0].astype(jnp.float32)
    square_sums = lax.psum(jnp.sum(stream_rows * stream_rows, axis=1), ("outer", "inner"))
    inverse_rms = lax.rsqrt(square_sums / D + 1e-05)
    gain = norm_gain[0].astype(jnp.float32)
    normed = (stream_rows * inverse_rms[:, None] * gain[None, :]).astype(jnp.bfloat16)
    weight_next = next_weight[0]
    summed = lax.psum_scatter(
        jnp.dot(normed, weight_next, preferred_element_type=jnp.float32).astype(jnp.bfloat16),
        ("outer", "inner"),
        scatter_dimension=0,
        tiled=True,
    )
    return (summed[None], received)


def solution(mesh):
    return jax.shard_map(
        body,
        mesh=mesh,
        in_specs=(
            P("section", ("outer", "inner"), None),
            P(),
            P("section", None, ("outer", "inner")),
            P("section", None, ("outer", "inner")),
            P("section", ("outer", "inner")),
            P("section", ("outer", "inner"), None),
        ),
        out_specs=(P("section", ("outer", "inner"), None), P("section", None, ("outer", "inner"))),
        check_vma=False,
    )
```

profile of v0, /device:TPU:24, one launch (start us, length us, event | category | flops | bytes accessed | tf_op | source)
XLA Modules:
  0.0 255.0 jit_solution(5510408127578099732)
XLA Ops:
  7.2 0.0 all-gather.2.cloned.1.call-start
  7.2 1.0 slice.18
  8.2 0.8 slice.16
  9.0 0.8 dynamic_slice.3
  9.8 0.9 broadcast_compare_fusion
  10.7 0.2 copy.10
  10.9 14.5 %all_gather.9 = bf16[512,256]{1,0:T(8,128)(2,1)S(1)} all-gather(bf16[128,256]{1,0:T(8,128)(2,1)S(1)} %slice.16), channel_id=1, replica_groups=mesh['section'=4,'outer'=2,'inner'=4] {'inner'}, dimensions={0}, use_global_device_ids=true | all-gather | bytes 327680 | tf_op jit(solution)/shard_map/all_gather | solution.py:24
  25.3 7.0 %all_gather.10 = bf16[1024,256]{1,0:T(8,128)(2,1)S(1)} all-gather(bf16[512,256]{1,0:T(8,128)(2,1)S(1)} %all_gather.9), channel_id=1, replica_groups=mesh['section'=4,'outer'=2,'inner'=4] {'outer'}, dimensions={0}, use_global_device_ids=true | all-gather | bytes 786432 | tf_op jit(solution)/shard_map/all_gather | solution.py:25
  32.4 0.8 fusion.11
  33.2 0.9 fusion.23
  34.0 1.6 fusion.34
  35.6 0.0 all-gather.2.cloned.1.call-update
  35.7 0.0 copy-start.1
  35.7 0.0 reduce-scatter.2.cloned.1.call-start
  35.7 49.5 %all-gather.2.cloned.1.call-done = bf16[1024,1024]{0,1:T(8,128)(2,1)} async-done(((bf16[128,1024]{0,1:T(8,128)(2,1)}), bf16[1024,1024]{0,1:T(8,128)(2,1)}) %all-gather.2.cloned.1.call-update) | async-done | bytes 2097168 | tf_op jit(solution)/shard_map/all_gather | solution.py:46
  85.3 8.6 %fusion.6 = bf16[1,1024,2048]{2,1,0:T(8,128)(2,1)S(1)} fusion(bf16[1,1024,2048]{2,1,0:T(8,128)(2,1)} %param.9, bf16[1024,1024]{0,1:T(8,128)(2,1)} %all-gather.2.cloned.1.call-done, bf16[1,1024,2048]{2,1,0:T(8,128)(2,1)} %param.8), kind=kOutput, calls=%fused_computation.9 | convolution fusion | flops 4301258752 | bytes 14680064 | tf_op jit(solution)/shard_map/dot_general | solution.py:45
  93.9 0.1 collective-permute-start
  94.0 0.0 copy-done.1
  94.0 47.9 %collective-permute-done = bf16[1,1024,2048]{2,1,0:T(8,128)(2,1)S(1)} collective-permute-done((bf16[1,1024,2048]{2,1,0:T(8,128)(2,1)S(1)}, bf16[1,1024,2048]{2,1,0:T(8,128)(2,1)S(1)}, u32[]{:S(2)}, u32[]{:S(2)}) %collective-permute-start) | collective-permute-done | bytes 4194336 | tf_op jit(solution)/shard_map/ppermute | solution.py:13
  141.9 0.0 copy-start
  141.9 1.9 copy-done
  143.8 0.9 fusion
  144.7 17.8 %psum.7 = f32[1024]{0:T(1024)S(1)} all-reduce(f32[1024]{0:T(1024)S(1)} %fusion), channel_id=1, replica_groups=mesh['section'=4,'outer'=2,'inner'=4] {'outer','inner'}, use_global_device_ids=true, to_apply=%region_3.4 | all-reduce | flops 1024 | bytes 8192 | tf_op jit(solution)/shard_map/psum | solution.py:53
  162.5 10.3 %fusion.16 = bf16[1024,1280]{1,0:T(8,128)(2,1)} fusion(bf16[1,2048,1280]{2,1,0:T(8,128)(2,1)} %param.11, bf16[1,1024,2048]{2,1,0:T(8,128)(2,1)} %copy-done, f32[2048]{0:T(1024)S(1)} %bitcast.66, f32[1024]{0:T(1024)S(1)} %add_rsqrt_fusion), kind=kOutput, calls=%fused_computation.20 | convolution fusion | flops 5378408448 | bytes 12070912 | tf_op jit(solution)/shard_map/dot_general | solution.py:59
  172.8 0.0 reduce-scatter.2.cloned.1.call-update
  172.8 70.6 %reduce-scatter.2.cloned.1.call-done = bf16[128,1280]{1,0:T(8,128)(2,1)} async-done(((bf16[1024,1280]{1,0:T(8,128)(2,1)}), bf16[128,1280]{1,0:T(8,128)(2,1)}) %reduce-scatter.2.cloned.1.call-update) | async-done | bytes 327696 | tf_op jit(solution)/shard_map/reduce_scatter | solution.py:58
  243.4 4.8 %copy.19 = bf16[1,1024,2048]{2,1,0:T(8,128)(2,1)} copy(bf16[1,1024,2048]{2,1,0:T(8,128)(2,1)} %copy-done) | data formatting | bytes 8388608
  (3 shorter events, 0.0 us)
Async XLA Ops:
  7.2 78.1 %all-gather.2.cloned.1.call-start = ((), (), s32[]{:S(2)}) async-start(), calls=%async_computation.1 | async-start | bytes 2359296 | tf_op jit(solution)/shard_map/all_gather | solution.py:46
  35.7 58.3 %copy-start.1 = (bf16[1,2048]{1,0:T(2,128)(2,1)S(1)}, bf16[1,2048]{1,0:T(2,128)(2,1)}, u32[]{:S(2)}) copy-start(bf16[1,2048]{1,0:T(2,128)(2,1)} %param.10) | copy-start | bytes 12292
  35.7 207.7 %reduce-scatter.2.cloned.1.call-start = ((), (), s32[]{:S(2)}) async-start(), calls=%async_computation.2 | async-start | bytes 2949120 | tf_op jit(solution)/shard_map/reduce_scatter | solution.py:58
  93.9 48.0 %collective-permute-start = (bf16[1,1024,2048]{2,1,0:T(8,128)(2,1)S(1)}, bf16[1,1024,2048]{2,1,0:T(8,128)(2,1)S(1)}, u32[]{:S(2)}, u32[]{:S(2)}) collective-permute-start(bf16[1,1024,2048]{2,1,0:T(8,128)(2,1)S(1)} %fusion.6), channel_id=1, source_target_pairs={{0,8},{8,16},{16,24},{24,0},{1,9},{9,17},{17,25},{25,1},{2,10},{10... | collective-permute-start | bytes 12582920 | tf_op jit(solution)/shard_map/ppermute | solution.py:13
  141.9 1.9 copy-start
Sparse Core Ops, SparseCore 0:
  35.8 49.4 all-gather.1
  172.9 70.4 reduce-scatter.1
where the time goes:
time: 259 us; the launch traced here: 255 us
  waiting for transfers between devices  168 us (65%)
  blocking collectives  39.3 us (15%)
  matrix products  21.3 us (8%)
  between operations  14.1 us (5%)
  local copies, waits for them, and re-layouts  9.46 us (4%)
  other arithmetic  2.65 us (1%)
    reduce_scatter x1, waiting for transfers between devices, body(): lax.psum_scatter(jnp.dot(normed, weight_next, preferred_element_type=jnp....  70.6 us
    all_gather x1, waiting for transfers between devices, body(): lax.all_gather(attended, ('outer', 'inner'), axis=0, tiled=True)  49.5 us
    ppermute x1, waiting for transfers between devices, from_behind(): lax.ppermute(value, axis, [(i, (i + by) % devices) for i in range(devices)])  47.9 us
    psum x1, blocking collectives, body(): lax.psum(jnp.sum(stream_rows * stream_rows, axis=1), ('outer', 'inner'))  17.8 us
    all_gather x1, blocking collectives, body(): group_rows = lax.all_gather(key_value, 'inner', axis=0, tiled=True)  14.5 us
    dot_general x1, matrix products, body(): jnp.dot(normed, weight_next, preferred_element_type=jnp.float32)  10.3 us
    dot_general x1, matrix products, body(): jnp.dot(lax.all_gather(attended, ('outer', 'inner'), axis=0, tiled=True),...  8.64 us
    all_gather x1, blocking collectives, body(): piece = lax.all_gather(group_rows, 'outer', axis=0, tiled=True)  7.03 us
  transfers between devices with their start and end apart: 3, of which 3 were waited for; matrix products, arithmetic and copies ran while one was open for 0% of the time, Pallas kernels for 0%

commit v1 on v0

v1 whole, which is shorter than its diff:
```python
import functools

import jax
import jax.numpy as jnp
from jax import lax
from jax.experimental import pallas as pl
from jax.experimental.pallas import tpu as pltpu
from jax.sharding import PartitionSpec as P

HD = 128
LANES = 128
MESH = pl.DeviceIdType.MESH


def kernel(
    sizes,
    proj_ref,
    pos_ref,
    w1_hbm,
    res_hbm,
    gain_ref,
    w2_hbm,
    out_ref,
    stream_hbm,
    w1,
    res,
    w2,
    kv,
    att,
    hid,
    st,
    part,
    from_outer,
    from_inner,
    load_sem,
    store_sem,
    kv_inner_send,
    kv_outer_send,
    kv_recv,
    att_inner_send,
    att_outer_send,
    att_recv,
    hid_send,
    st_recv,
    px_send,
    px_recv,
    pz_send,
    pz_recv,
):
    sections, outers, inners, width = sizes
    shards = outers * inners
    sec = lax.axis_index("section")
    out = lax.axis_index("outer")
    inn = lax.axis_index("inner")
    me = out * inners + inn
    rows = proj_ref.shape[1]
    qw = proj_ref.shape[2]
    heads = (qw - 2 * HD) // HD
    cols = w1.shape[1]

    def shard_of(a, b):
        return lax.rem(out + a, outers) * inners + lax.rem(inn + b, inners)

    def outer_peer(a):
        return (sec, lax.rem(out + a, outers), inn)

    def inner_peer(b):
        return (sec, out, lax.rem(inn + b, inners))

    behind = (lax.rem(sec + sections - 1, sections), out, inn)
    ahead = (lax.rem(sec + 1, sections), out, inn)

    load_w1 = pltpu.make_async_copy(w1_hbm.at[0], w1, load_sem.at[0])
    load_res = pltpu.make_async_copy(res_hbm.at[0], res, load_sem.at[1])
    load_w2 = pltpu.make_async_copy(w2_hbm.at[0], w2, load_sem.at[2])
    load_w1.start()
    load_res.start()
    load_w2.start()

    barrier = pltpu.get_barrier_semaphore()
    peers = [outer_peer(a) for a in range(1, outers)]
    peers += [inner_peer(b) for b in range(1, inners)]
    peers += [behind, ahead]
    for peer in peers:
        pl.semaphore_signal(barrier, inc=1, device_id=peer, device_id_type=MESH)
    pl.semaphore_wait(barrier, len(peers))

    def remote(src, dst, send, recv, peer):
        return pltpu.make_async_remote_copy(
            src_ref=src,
            dst_ref=dst,
            send_sem=send,
            recv_sem=recv,
            device_id=peer,
            device_id_type=MESH,
        )

    def to_inner(buf, b, send, recv):
        return remote(buf.at[me], buf.at[me], send.at[b], recv.at[me], inner_peer(b))

    def to_outer(buf, a, b, send, recv):
        slot = shard_of(0, b)
        return remote(
            buf.at[slot], buf.at[slot], send.at[a, b], recv.at[slot], outer_peer(a)
        )

    def arrive(buf, slot, send, recv):
        remote(buf.at[slot], buf.at[slot], send.at[0], recv.at[slot], ahead).wait_recv()

    kv[me] = proj_ref[0, :, heads * HD :]
    for b in range(1, inners):
        to_inner(kv, b, kv_inner_send, kv_recv).start()
    for a in range(1, outers):
        to_outer(kv, a, 0, kv_outer_send, kv_recv).start()
    for b in range(1, inners):
        arrive(kv, shard_of(0, b), kv_inner_send, kv_recv)
        for a in range(1, outers):
            to_outer(kv, a, b, kv_outer_send, kv_recv).start()
    for b in range(inners):
        for a in range(1, outers):
            arrive(kv, shard_of(a, b), kv_inner_send, kv_recv)

    key_pos = pos_ref[...]
    own_pos = pos_ref[:, pl.ds(pl.multiple_of(me * rows, rows), rows)]
    own_col = jnp.transpose(
        jnp.broadcast_to(own_pos.astype(jnp.float32), (LANES, rows))
    )[:, :1]
    own_col = own_col.astype(jnp.int32)
    scale = HD ** (-0.5)

    def head_step(h, carry):
        at = pl.ds(pl.multiple_of(h * HD, HD), HD)
        queries = proj_ref[0, :, at]
        keys = kv[:, :, :HD].reshape(shards * rows, HD)
        values = kv[:, :, HD:].reshape(shards * rows, HD)
        scores = (
            lax.dot_general(
                queries, keys, (((1,), (1,)), ((), ())), preferred_element_type=jnp.float32
            )
            * scale
        )
        visible = key_pos <= own_col
        masked = jnp.where(visible, scores, -1e30)
        top = jnp.max(masked, axis=1, keepdims=True)
        weights = jnp.where(visible, jnp.exp(masked - top), 0.0)
        total = jnp.sum(weights, axis=1, keepdims=True)
        mixed = jnp.dot(weights.astype(jnp.bfloat16), values, preferred_element_type=jnp.float32)
        att[me, :, at] = (mixed / total).astype(jnp.bfloat16)
        return carry

    lax.fori_loop(0, heads, head_step, 0)

    for b in range(1, inners):
        to_inner(att, b, att_inner_send, att_recv).start()
    for a in range(1, outers):
        to_outer(att, a, 0, att_outer_send, att_recv).start()
    load_w1.wait()
    load_res.wait()
    load_w2.wait()

    def place(k):
        middle = k <= (inners - 1) * outers
        a = jnp.where(
            k == 0, 0, jnp.where(middle, lax.rem(k + outers - 1, outers), k - (inners - 1) * outers)
        )
        b = jnp.where(k == 0, 0, jnp.where(middle, (k + outers - 1) // outers, 0))
        return a, b

    def shift(slot):
        return remote(hid.at[slot], st.at[slot], hid_send.at[slot], st_recv.at[slot], ahead)

    def store(slot):
        at = pl.ds(pl.multiple_of(slot * rows, rows), rows)
        return pltpu.make_async_copy(st.at[slot], stream_hbm.at[0, at, :], store_sem.at[slot])

    def exchange(a, b):
        return remote(
            part.at[shard_of(a, b)],
            from_outer.at[a, b],
            px_send.at[a, b],
            px_recv.at[a, b],
            outer_peer(a),
        )

    def scatter(b):
        return remote(
            part.at[shard_of(0, b)], from_inner.at[b], pz_send.at[b], pz_recv.at[b], inner_peer(b)
        )

    def first(k):
        a, b = place(k)
        slot = shard_of(a, b)

        @pl.when(k > 0)
        def _():
            arrive(att, slot, att_inner_send, att_recv)

            @pl.when(a == 0)
            def _():
                for c in range(1, outers):
                    to_outer(att, c, b, att_outer_send, att_recv).start()

        at = pl.ds(pl.multiple_of(slot * rows, rows), rows)
        product = jnp.dot(att[slot], w1[...], preferred_element_type=jnp.float32)
        hid[slot] = (res[at, :].astype(jnp.float32) + product).astype(jnp.bfloat16)
        shift(slot).start()

    def second(k):
        a, b = place(k)
        slot = shard_of(a, b)
        shift(slot).wait_recv()
        store(slot).start()
        values = st[slot].astype(jnp.float32)
        scaled = (values * gain_ref[...].astype(jnp.float32)).astype(jnp.bfloat16)
        part[slot, :, :qw] = jnp.dot(
            scaled, w2[...], preferred_element_type=jnp.float32
        ).astype(jnp.bfloat16)
        squares = values * values
        lanes = squares[:, :LANES]
        for j in range(1, cols // LANES):
            lanes += squares[:, j * LANES : (j + 1) * LANES]
        part[slot, :, qw:] = lanes.astype(jnp.bfloat16)

        @pl.when(a > 0)
        def _():
            exchange(a, b).start()

    def combine(b):
        slot = shard_of(0, b)
        total = part[slot].astype(jnp.float32)
        for a in range(1, outers):
            exchange(a, b).wait_recv()
            total += from_outer[a, b].astype(jnp.float32)
        part[slot] = total.astype(jnp.bfloat16)
        scatter(b).start()

    lag = max(1, shards // 2)

    def step(k, carry):
        @pl.when(k < shards)
        def _():
            first(k)

        @pl.when(k >= lag)
        def _():
            second(k - lag)

            for b in range(1, inners):

                @pl.when(k - lag == min((b + 1) * outers, shards - 1))
                def _():
                    combine(b)

        return carry

    lax.fori_loop(0, shards + lag, step, 0)

    total = part[me].astype(jnp.float32)
    for a in range(1, outers):
        exchange(a, 0).wait_recv()
        total += from_outer[a, 0].astype(jnp.float32)
    for b in range(1, inners):
        scatter(b).wait_recv()
        total += from_inner[b].astype(jnp.float32)
    mean = jnp.sum(total[:, qw:], axis=1, keepdims=True) / width
    out_ref[0] = (total[:, :qw] * lax.rsqrt(mean + 1e-05)).astype(jnp.bfloat16)

    for b in range(1, inners):
        to_inner(kv, b, kv_inner_send, kv_recv).wait_send()
        to_inner(att, b, att_inner_send, att_recv).wait_send()
        scatter(b).wait_send()
    for a in range(1, outers):
        for b in range(inners):
            to_outer(kv, a, b, kv_outer_send, kv_recv).wait_send()
            to_outer(att, a, b, att_outer_send, att_recv).wait_send()
            exchange(a, b).wait_send()

    def drain(slot, carry):
        shift(slot).wait_send()
        store(slot).wait()
        return carry

    lax.fori_loop(0, shards, drain, 0)


def body(mesh, projected, positions, out_weight, residual, norm_gain, next_weight):
    sections, outers, inners = (mesh.shape[n] for n in ("section", "outer", "inner"))
    shards = outers * inners
    rows, qw = projected.shape[1:]
    inner_width, cols = out_weight.shape[1:]
    seq = positions.shape[0]
    wide = qw + LANES
    bf16 = jnp.bfloat16
    dma = pltpu.SemaphoreType.DMA
    vmem = pl.BlockSpec(memory_space=pltpu.VMEM)
    hbm = pl.BlockSpec(memory_space=pl.ANY)
    return pl.pallas_call(
        functools.partial(kernel, (sections, outers, inners, cols * shards)),
        out_shape=(
            jax.ShapeDtypeStruct((1, rows, qw), bf16),
            jax.ShapeDtypeStruct((1, seq, cols), bf16),
        ),
        in_specs=[vmem, vmem, hbm, hbm, vmem, hbm],
        out_specs=(vmem, hbm),
        scratch_shapes=[
            pltpu.VMEM((inner_width, cols), bf16),
            pltpu.VMEM((seq, cols), bf16),
            pltpu.VMEM((cols, qw), bf16),
            pltpu.VMEM((shards, rows, 2 * HD), bf16),
            pltpu.VMEM((shards, rows, inner_width), bf16),
            pltpu.VMEM((shards, rows, cols), bf16),
            pltpu.VMEM((shards, rows, cols), bf16),
            pltpu.VMEM((shards, rows, wide), bf16),
            pltpu.VMEM((outers, inners, rows, wide), bf16),
            pltpu.VMEM((inners, rows, wide), bf16),
            dma((3,)),
            dma((shards,)),
            dma((inners,)),
            dma((outers, inners)),
            dma((shards,)),
            dma((inners,)),
            dma((outers, inners)),
            dma((shards,)),
            dma((shards,)),
            dma((shards,)),
            dma((outers, inners)),
            dma((outers, inners)),
            dma((inners,)),
            dma((inners,)),
        ],
        compiler_params=pltpu.CompilerParams(
            collective_id=0, has_side_effects=True, vmem_limit_bytes=63 * 1024 * 1024
        ),
    )(
        projected,
        positions.reshape(1, seq),
        out_weight,
        residual,
        norm_gain.reshape(1, cols),
        next_weight,
    )


def solution(mesh):
    return jax.shard_map(
        functools.partial(body, mesh),
        mesh=mesh,
        in_specs=(
            P("section", ("outer", "inner"), None),
            P(),
            P("section", None, ("outer", "inner")),
            P("section", None, ("outer", "inner")),
            P("section", ("outer", "inner")),
            P("section", ("outer", "inner"), None),
        ),
        out_specs=(P("section", ("outer", "inner"), None), P("section", None, ("outer", "inner"))),
        check_vma=False,
    )
```

time: 259 us -> 115 us (0.44); the launches traced: 255 us -> 115 us
  waiting for transfers between devices: 168 us -> 0 us
  Pallas kernels: 0 us -> 107 us
  blocking collectives: 39.3 us -> 0 us
  matrix products: 21.3 us -> 0 us
  between operations: 14.1 us -> 0.64 us
  local copies, waits for them, and re-layouts: 9.46 us -> 6.51 us
  other arithmetic: 2.65 us -> 0 us
    pallas_call x0 -> x1, Pallas kernels: none -> 107 us  [body(): pl.pallas_call(functools.partial(kernel, (sections, outers, inners, cols...]
    reduce_scatter x1 -> x0, waiting for transfers between devices: 70.6 us -> none  [body(): lax.psum_scatter(jnp.dot(normed, weight_next, preferred_element_type=jnp....]
    all_gather x1 -> x0, waiting for transfers between devices: 49.5 us -> none  [body(): lax.all_gather(attended, ('outer', 'inner'), axis=0, tiled=True)]
    ppermute x1 -> x0, waiting for transfers between devices: 47.9 us -> none  [from_behind(): lax.ppermute(value, axis, [(i, (i + by) % devices) for i in range(devices)])]
    all_gather x2 -> x0, blocking collectives: 21.5 us -> none  [the longest x1 14.5 us: body(): group_rows = lax.all_gather(key_value, 'inner', axis=0, tiled=True)]
    dot_general x4 -> x0, matrix products: 21.3 us -> none  [the longest x1 10.3 us: body(): jnp.dot(normed, weight_next, preferred_element_type=jnp.float32)]
    psum x1 -> x0, blocking collectives: 17.8 us -> none  [body(): lax.psum(jnp.sum(stream_rows * stream_rows, axis=1), ('outer', 'inner'))]
    unnamed x5 -> x2, local copies, waits for them, and re-layouts: 6.72 us -> 6.51 us
  transfers between devices with their start and end apart: 3 -> 0, of which waited for: 3 -> 0; matrix products, arithmetic and copies ran while one was open for 0% -> 0% of each run, Pallas kernels for 0% -> 0%
where the time goes in v1:
time: 115 us
  Pallas kernels  107 us (93%)
  local copies, waits for them, and re-layouts  6.51 us (6%)
    pallas_call x1, Pallas kernels, body(): pl.pallas_call(functools.partial(kernel, (sections, outers, inners, cols...  107 us
    unnamed x2, local copies, waits for them, and re-layouts  6.51 us

profile of v1, /device:TPU:24, one launch (start us, length us, event | category | flops | bytes accessed | tf_op | source)
XLA Modules:
  0.0 114.6 jit_solution(8909218918126092508)
XLA Ops:
  0.6 107.4 %shard_map.77 = (bf16[1,128,1280]{2,1,0:T(8,128)(2,1)}, bf16[1,1024,2048]{2,1,0:T(8,128)(2,1)}) custom-call(bf16[1,128,1280]{2,1,0:T(8,128)(2,1)} %proj_ref.1, s32[1,1024]{1,0:T(1,128)} %bitcast.1, bf16[1,1024,2048]{2,1,0:T(8,128)(2,1)} %w1_hbm.1, bf16[1,1024,2048]{2,1,0:T(8,128)(2,1)} %res_hbm.1, bf16[1,2048]{1,0:T(2,128)(2,1)} %gain_ref.1, ...), custom_call_target="tpu_custom_call" | custom-call | tf_op jit(solution)/shard_map/pallas_call | solution.py:297
  108.0 1.7 %copy.10 = bf16[1,128,1280]{2,1,0:T(8,128)(2,1)} copy(bf16[1,128,1280]{2,1,0:T(8,128)(2,1)} %get-tuple-element.4) | data formatting | bytes 655360
  109.8 4.8 %copy.11 = bf16[1,1024,2048]{2,1,0:T(8,128)(2,1)} copy(bf16[1,1024,2048]{2,1,0:T(8,128)(2,1)} %get-tuple-element.5) | data formatting | bytes 8388608

commit v2 on v1

--- a/solution.py
+++ b/solution.py
@@ -58,8 +58,16 @@
     heads = (qw - 2 * HD) // HD
     cols = w1.shape[1]
 
-    def shard_of(a, b):
-        return lax.rem(out + a, outers) * inners + lax.rem(inn + b, inners)
+    last = inners - 1
+    near = jnp.minimum(inn, last - inn)
+
+    def nearest(t):
+        paired = jnp.where(lax.rem(t, 2) == 1, inn - (t + 1) // 2, inn + (t + 1) // 2)
+        single = jnp.where(inn == near, inn + t - near, inn - t + near)
+        return jnp.where(t <= 2 * near, paired, single)
+
+    def shard_of(a, t):
+        return lax.rem(out + a, outers) * inners + nearest(t)
 
     def outer_peer(a):
         return (sec, lax.rem(out + a, outers), inn)
@@ -95,8 +103,23 @@
             device_id_type=MESH,
         )
 
-    def to_inner(buf, b, send, recv):
-        return remote(buf.at[me], buf.at[me], send.at[b], recv.at[me], inner_peer(b))
+    def along(buf, t, send, recv, up):
+        slot = shard_of(0, t)
+        peer = (sec, out, inn + 1 if up else inn - 1)
+        return remote(buf.at[slot], buf.at[slot], send.at[int(up), t], recv.at[slot], peer)
+
+    def relay(buf, t, send, recv, done=False):
+        origin = nearest(t)
+
+        @pl.when(jnp.logical_and(origin <= inn, inn < last))
+        def _():
+            copy = along(buf, t, send, recv, True)
+            copy.wait_send() if done else copy.start()
+
+        @pl.when(jnp.logical_and(origin >= inn, inn > 0))
+        def _():
+            copy = along(buf, t, send, recv, False)
+            copy.wait_send() if done else copy.start()
 
     def to_outer(buf, a, b, send, recv):
         slot = shard_of(0, b)
@@ -105,15 +128,15 @@
         )
 
     def arrive(buf, slot, send, recv):
-        remote(buf.at[slot], buf.at[slot], send.at[0], recv.at[slot], ahead).wait_recv()
+        remote(buf.at[slot], buf.at[slot], send.at[0, 0], recv.at[slot], ahead).wait_recv()
 
     kv[me] = proj_ref[0, :, heads * HD :]
-    for b in range(1, inners):
-        to_inner(kv, b, kv_inner_send, kv_recv).start()
+    relay(kv, 0, kv_inner_send, kv_recv)
     for a in range(1, outers):
         to_outer(kv, a, 0, kv_outer_send, kv_recv).start()
     for b in range(1, inners):
         arrive(kv, shard_of(0, b), kv_inner_send, kv_recv)
+        relay(kv, b, kv_inner_send, kv_recv)
         for a in range(1, outers):
             to_outer(kv, a, b, kv_outer_send, kv_recv).start()
     for b in range(inners):
@@ -150,21 +173,25 @@
 
     lax.fori_loop(0, heads, head_step, 0)
 
-    for b in range(1, inners):
-        to_inner(att, b, att_inner_send, att_recv).start()
+    relay(att, 0, att_inner_send, att_recv)
     for a in range(1, outers):
         to_outer(att, a, 0, att_outer_send, att_recv).start()
     load_w1.wait()
     load_res.wait()
     load_w2.wait()
 
+    tail = 2 + (inners - 2) * outers
+
     def place(k):
-        middle = k <= (inners - 1) * outers
-        a = jnp.where(
-            k == 0, 0, jnp.where(middle, lax.rem(k + outers - 1, outers), k - (inners - 1) * outers)
-        )
-        b = jnp.where(k == 0, 0, jnp.where(middle, (k + outers - 1) // outers, 0))
-        return a, b
+        turn, rank = lax.rem(k + 2 * outers - 2, outers), 2 + (k - 2) // outers
+        left = k - tail
+        a = jnp.where(k < tail, turn, jnp.where(left < outers - 1, 1 + left, 2 + left - outers))
+        t = jnp.where(
+            k < tail,
+            jnp.where(turn == 0, rank, rank - 1),
+            jnp.where(left < outers - 1, inners - 1, 0),
+        )
+        return jnp.where(k < 2, 0, a), jnp.where(k < 2, k, t)
 
     def shift(slot):
         return remote(hid.at[slot], st.at[slot], hid_send.at[slot], st_recv.at[slot], ahead)
@@ -184,8 +211,16 @@
 
     def scatter(b):
         return remote(
-            part.at[shard_of(0, b)], from_inner.at[b], pz_send.at[b], pz_recv.at[b], inner_peer(b)
-        )
+            part.at[shard_of(0, b)],
+            from_inner.at[inn],
+            pz_send.at[b],
+            pz_recv.at[inn],
+            (sec, out, nearest(b)),
+        )
+
+    def gathered(b):
+        peer = nearest(b)
+        return remote(part.at[me], from_inner.at[peer], pz_send.at[0], pz_recv.at[peer], ahead)
 
     def first(k):
         a, b = place(k)
@@ -197,6 +232,7 @@
 
             @pl.when(a == 0)
             def _():
+                relay(att, b, att_inner_send, att_recv)
                 for c in range(1, outers):
                     to_outer(att, c, b, att_outer_send, att_recv).start()
 
@@ -234,7 +270,7 @@
         part[slot] = total.astype(jnp.bfloat16)
         scatter(b).start()
 
-    lag = max(1, shards // 2)
+    lag = max(1, 3 * shards // 8)
 
     def step(k, carry):
         @pl.when(k < shards)
@@ -247,7 +283,7 @@
 
             for b in range(1, inners):
 
-                @pl.when(k - lag == min((b + 1) * outers, shards - 1))
+                @pl.when(k - lag == min(2 + b * outers, tail + outers - 1))
                 def _():
                     combine(b)
 
@@ -260,20 +296,22 @@
         exchange(a, 0).wait_recv()
         total += from_outer[a, 0].astype(jnp.float32)
     for b in range(1, inners):
-        scatter(b).wait_recv()
-        total += from_inner[b].astype(jnp.float32)
+        gathered(b).wait_recv()
+        total += from_inner[nearest(b)].astype(jnp.float32)
     mean = jnp.sum(total[:, qw:], axis=1, keepdims=True) / width
     out_ref[0] = (total[:, :qw] * lax.rsqrt(mean + 1e-05)).astype(jnp.bfloat16)
 
     for b in range(1, inners):
-        to_inner(kv, b, kv_inner_send, kv_recv).wait_send()
-        to_inner(att, b, att_inner_send, att_recv).wait_send()
         scatter(b).wait_send()
     for a in range(1, outers):
         for b in range(inners):
             to_outer(kv, a, b, kv_outer_send, kv_recv).wait_send()
             to_outer(att, a, b, att_outer_send, att_recv).wait_send()
             exchange(a, b).wait_send()
+
+    for b in range(inners):
+        relay(kv, b, kv_inner_send, kv_recv, True)
+        relay(att, b, att_inner_send, att_recv, True)
 
     def drain(slot, carry):
         shift(slot).wait_send()
@@ -315,10 +353,10 @@
             pltpu.VMEM((inners, rows, wide), bf16),
             dma((3,)),
             dma((shards,)),
-            dma((inners,)),
+            dma((2, inners)),
             dma((outers, inners)),
             dma((shards,)),
-            dma((inners,)),
+            dma((2, inners)),
             dma((outers, inners)),
             dma((shards,)),
             dma((shards,)),

time: 115 us -> 99 us (0.86)
  Pallas kernels: 107 us -> 91.6 us
    pallas_call x1, Pallas kernels: 107 us -> 91.6 us  [body(): pl.pallas_call(functools.partial(kernel, (sections, outers, inners, cols...]
where the time goes in v2:
time: 99 us; the launch traced here: 98.8 us
  Pallas kernels  91.6 us (93%)
  local copies, waits for them, and re-layouts  6.51 us (7%)
    pallas_call x1, Pallas kernels, body(): pl.pallas_call(functools.partial(kernel, (sections, outers, inners, cols...  91.6 us
    unnamed x2, local copies, waits for them, and re-layouts  6.51 us

profile of v2, /device:TPU:24, one launch (start us, length us, event | category | flops | bytes accessed | tf_op | source)
XLA Modules:
  0.0 98.8 jit_solution(3020052730807073664)
XLA Ops:
  0.6 91.6 %shard_map.77 = (bf16[1,128,1280]{2,1,0:T(8,128)(2,1)}, bf16[1,1024,2048]{2,1,0:T(8,128)(2,1)}) custom-call(bf16[1,128,1280]{2,1,0:T(8,128)(2,1)} %proj_ref.1, s32[1,1024]{1,0:T(1,128)} %bitcast.1, bf16[1,1024,2048]{2,1,0:T(8,128)(2,1)} %w1_hbm.1, bf16[1,1024,2048]{2,1,0:T(8,128)(2,1)} %res_hbm.1, bf16[1,2048]{1,0:T(2,128)(2,1)} %gain_ref.1, ...), custom_call_target="tpu_custom_call" | custom-call | tf_op jit(solution)/shard_map/pallas_call | solution.py:335
  92.3 1.7 %copy.10 = bf16[1,128,1280]{2,1,0:T(8,128)(2,1)} copy(bf16[1,128,1280]{2,1,0:T(8,128)(2,1)} %get-tuple-element.4) | data formatting | bytes 655360
  94.0 4.8 %copy.11 = bf16[1,1024,2048]{2,1,0:T(8,128)(2,1)} copy(bf16[1,1024,2048]{2,1,0:T(8,128)(2,1)} %get-tuple-element.5) | data formatting | bytes 8388608

commit v3 on v2

--- a/solution.py
+++ b/solution.py
@@ -1,4 +1,5 @@
 import functools
+import math
 
 import jax
 import jax.numpy as jnp
@@ -180,18 +181,18 @@
     load_res.wait()
     load_w2.wait()
 
-    tail = 2 + (inners - 2) * outers
+    others = outers - 1
 
     def place(k):
-        turn, rank = lax.rem(k + 2 * outers - 2, outers), 2 + (k - 2) // outers
-        left = k - tail
-        a = jnp.where(k < tail, turn, jnp.where(left < outers - 1, 1 + left, 2 + left - outers))
-        t = jnp.where(
-            k < tail,
-            jnp.where(turn == 0, rank, rank - 1),
-            jnp.where(left < outers - 1, inners - 1, 0),
-        )
-        return jnp.where(k < 2, 0, a), jnp.where(k < 2, k, t)
+        beyond = jnp.maximum(k - inners, 0)
+        block = beyond // others
+        t = jnp.where(block < inners - 2, 2 + block, inners - 1 - block)
+        inside = k < inners
+        return jnp.where(inside, 0, 1 + lax.rem(beyond, others)), jnp.where(inside, k, t)
+
+    def ready(t):
+        block = t - 2 if t > 1 else inners - 2
+        return inners + (block + 2) * others - 1
 
     def shift(slot):
         return remote(hid.at[slot], st.at[slot], hid_send.at[slot], st_recv.at[slot], ahead)
@@ -270,7 +271,7 @@
         part[slot] = total.astype(jnp.bfloat16)
         scatter(b).start()
 
-    lag = max(1, 3 * shards // 8)
+    lag = max(1, shards // 4)
 
     def step(k, carry):
         @pl.when(k < shards)
@@ -283,7 +284,7 @@
 
             for b in range(1, inners):
 
-                @pl.when(k - lag == min(2 + b * outers, tail + outers - 1))
+                @pl.when(k - lag == ready(b))
                 def _():
                     combine(b)
 
@@ -332,6 +333,20 @@
     dma = pltpu.SemaphoreType.DMA
     vmem = pl.BlockSpec(memory_space=pltpu.VMEM)
     hbm = pl.BlockSpec(memory_space=pl.ANY)
+    shapes = (
+        (inner_width, cols),
+        (seq, cols),
+        (cols, qw),
+        (shards, rows, 2 * HD),
+        (shards, rows, inner_width),
+        (shards, rows, cols),
+        (shards, rows, cols),
+        (shards, rows, wide),
+        (outers, inners, rows, wide),
+        (inners, rows, wide),
+    )
+    scratch = sum(2 * math.prod(shape) for shape in shapes)
+    grant = min(63, scratch // 2**20 + 18) * 2**20
     return pl.pallas_call(
         functools.partial(kernel, (sections, outers, inners, cols * shards)),
         out_shape=(
@@ -341,16 +356,7 @@
         in_specs=[vmem, vmem, hbm, hbm, vmem, hbm],
         out_specs=(vmem, hbm),
         scratch_shapes=[
-            pltpu.VMEM((inner_width, cols), bf16),
-            pltpu.VMEM((seq, cols), bf16),
-            pltpu.VMEM((cols, qw), bf16),
-            pltpu.VMEM((shards, rows, 2 * HD), bf16),
-            pltpu.VMEM((shards, rows, inner_width), bf16),
-            pltpu.VMEM((shards, rows, cols), bf16),
-            pltpu.VMEM((shards, rows, cols), bf16),
-            pltpu.VMEM((shards, rows, wide), bf16),
-            pltpu.VMEM((outers, inners, rows, wide), bf16),
-            pltpu.VMEM((inners, rows, wide), bf16),
+            *(pltpu.VMEM(shape, bf16) for shape in shapes),
             dma((3,)),
             dma((shards,)),
             dma((2, inners)),
@@ -367,7 +373,7 @@
             dma((inners,)),
         ],
         compiler_params=pltpu.CompilerParams(
-            collective_id=0, has_side_effects=True, vmem_limit_bytes=63 * 1024 * 1024
+            collective_id=0, has_side_effects=True, vmem_limit_bytes=grant
         ),
     )(
         projected,

time: 99 us -> 91.5 us (0.924)
  the two profiles are of different devices: /device:TPU:24 before, /device:TPU:0 now
where the time goes in v3:
time: 91.5 us; the launch traced here: 91.3 us
  Pallas kernels  85.6 us (94%)
  local copies, waits for them, and re-layouts  5.09 us (6%)
    pallas_call x1, Pallas kernels, body(): pl.pallas_call(functools.partial(kernel, (sections, outers, inners, cols...  85.6 us
    unnamed x8, local copies, waits for them, and re-layouts  5.09 us

profile of v3, /device:TPU:0, one launch (start us, length us, event | category | flops | bytes accessed | tf_op | source)
XLA Modules:
  0.0 91.3 jit_solution(14791459458954307019)
XLA Ops:
  0.6 0.0 copy-start
  0.6 1.0 %copy-done = bf16[1,128,1280]{2,1,0:T(8,128)(2,1)S(1)} copy-done((bf16[1,128,1280]{2,1,0:T(8,128)(2,1)S(1)}, bf16[1,128,1280]{2,1,0:T(8,128)(2,1)}, u32[]{:S(2)}) %copy-start) | copy-done | bytes 327704
  1.6 0.0 copy-start.1
  1.6 0.7 copy-done.1
  2.3 0.0 copy-start.2
  2.3 0.7 copy-done.2
  3.0 85.6 %shard_map.77 = (bf16[1,128,1280]{2,1,0:T(8,128)(2,1)S(1)}, bf16[1,1024,2048]{2,1,0:T(8,128)(2,1)S(1)}) custom-call(bf16[1,128,1280]{2,1,0:T(8,128)(2,1)S(1)} %copy-done, s32[1,1024]{1,0:T(1,128)S(1)} %bitcast.1, bf16[1,1024,2048]{2,1,0:T(8,128)(2,1)} %w1_hbm.1, bf16[1,1024,2048]{2,1,0:T(8,128)(2,1)} %res_hbm.1, bf16[1,2048]{1,0:T(2,128)(2,1)S(1)} %copy-done.1, ...), custom_call_target="tpu_custom_call" | custom-call | tf_op jit(solution)/shard_map/pallas_call | solution.py:350
  88.6 0.7 copy.10
  89.3 2.0 %copy.11 = bf16[1,1024,2048]{2,1,0:T(8,128)(2,1)} copy(bf16[1,1024,2048]{2,1,0:T(8,128)(2,1)S(1)} %get-tuple-element.5) | data formatting | bytes 8388608
Async XLA Ops:
  0.6 1.0 %copy-start = (bf16[1,128,1280]{2,1,0:T(8,128)(2,1)S(1)}, bf16[1,128,1280]{2,1,0:T(8,128)(2,1)}, u32[]{:S(2)}) copy-start(bf16[1,128,1280]{2,1,0:T(8,128)(2,1)} %proj_ref.1) | copy-start | bytes 983044
  1.6 0.7 copy-start.1
  2.3 0.7 copy-start.2
